TPU v7x, 32 devices: a whole 2x2x4 slice. The times are simulated.
32 devices in a mesh: prow: 8 (over y, x, core), pcol: 4 (over z).
Axes of the slice: x: 2, y: 2, z: 4, core: 2. Of those that a mesh axis runs over, the one named last changes fastest.
Arguments:
- inverse_trailing: bfloat16 [18432, 18432], P('prow', 'pcol'), may hold values from -6 to 6
- panel: bfloat16 [18432, 256], P('prow'), may hold values from -0.0625 to 0.0625
- supernode_inverse: float32 [256, 256], replicated, may hold values from -6 to 6
- block_live: int32 [72], replicated, may hold values from 0 to 1, as said below
Outputs:
- column_inverse: float32 [18432, 256], P('prow')
- diagonal_inverse: float32 [256, 256], replicated
Inputs may be any that keep to these rules, and one draw needn't show every extreme that they name: Each aligned group of 9 consecutive block rows (the rows of one index of prow) holds at least one block row with block_live 1.
All inputs are finite; a program needn't handle non-finite values.
Results may differ from a plain program's by a relative error of at most 0.0003.
Values may be sent and summed in bfloat16 or wider, within the bound.
No kernel may reach another device: no remote copies, remote signals or barrier semaphores. Data moves between devices by JAX's collectives and lax.ppermute only.
A program may use at most 128 MiB of HBM per device.

v0:
```python
import jax
import jax.numpy as jnp
from jax import lax
from jax.sharding import PartitionSpec as P


def from_root(block, axis, source):
    block = jnp.where(lax.axis_index(axis) == source, block, jnp.zeros_like(block))
    return lax.psum(block, axis)


def per_device(inverse_trailing, panel, supernode_inverse, block_live):
    rows_dev = panel.shape[0]
    width = panel.shape[1]
    col_count = inverse_trailing.shape[1]
    ratio = lax.axis_size("prow") // lax.axis_size("pcol")
    row_index = lax.axis_index("prow")
    col_index = lax.axis_index("pcol")
    live_all = jnp.repeat(block_live, width)
    col_live = lax.dynamic_slice_in_dim(live_all, col_index * col_count, col_count).astype(
        jnp.float32
    )
    row_live = lax.dynamic_slice_in_dim(live_all, row_index * rows_dev, rows_dev).astype(
        jnp.float32
    )
    partial_sum = jnp.zeros((rows_dev, width), jnp.float32)
    for half in range(ratio):
        received = from_root(panel, "prow", col_index * ratio + half)
        half_live = col_live[half * rows_dev : (half + 1) * rows_dev]
        masked_half = (received.astype(jnp.float32) * half_live[:, None]).astype(jnp.bfloat16)
        tile_cols = inverse_trailing[:, half * rows_dev : (half + 1) * rows_dev]
        partial_sum = partial_sum + jnp.dot(
            tile_cols, masked_half, preferred_element_type=jnp.float32
        )
    local_panel = panel.astype(jnp.float32) * row_live[:, None]
    contract_rows = (((0,), (0,)), ((), ()))
    total = lax.psum(partial_sum, "pcol")
    column_inverse = -total * row_live[:, None]
    term = lax.dot_general(
        local_panel, column_inverse, contract_rows, precision=lax.Precision.HIGHEST
    )
    diag_total = lax.psum(term, "prow")
    diagonal_inverse = supernode_inverse - diag_total
    return (column_inverse, diagonal_inverse)


def solution(mesh):
    in_specs = (P("prow", "pcol"), P("prow", None), P(), P())
    out_specs = (P("prow", None), P())
    return jax.shard_map(
        per_device, mesh=mesh, in_specs=in_specs, out_specs=out_specs, check_vma=False
    )
```

profile of v0, /device:TPU:0, one launch (start us, length us, event | category | flops | bytes accessed | tf_op | source)
XLA Modules:
  0.0 254.0 jit_solution(5009432006979550034)
XLA Ops:
  7.2 0.0 copy-start
  7.2 0.0 all-reduce.9.cloned.1.call-start
  7.2 2.8 %broadcast_select_fusion.1 = (bf16[2304,256]{1,0:T(8,128)(2,1)}, bf16[2304,256]{1,0:T(8,128)(2,1)}) fusion(bf16[2304,256]{1,0:T(8,128)(2,1)} %param.5, pred[]{:T(512)S(6)} %eq.6, pred[]{:T(512)S(6)} %eq.7), kind=kLoop, calls=%fused_computation.16 | loop fusion | flops 1179648 | bytes 3538946 | tf_op jit(solution)/shard_map/jit(_where)/select_n | solution.py:8
  10.1 0.0 all-reduce.9.cloned.1.call-update
  10.1 0.0 all-reduce.5.cloned.1.call-start
  10.2 0.0 copy-done
  10.2 0.1 broadcast_bitcast_fusion
  10.3 0.1 dynamic-slice_convert_fusion
  10.4 67.3 %all-reduce.9.cloned.1.call-done = (bf16[2304,256]{1,0:T(8,128)(2,1)}, bf16[2304,256]{1,0:T(8,128)(2,1)}) async-done(((bf16[2304,256]{1,0:T(8,128)(2,1)}, bf16[2304,256]{1,0:T(8,128)(2,1)}), (bf16[2304,256]{1,0:T(8,128)(2,1)}, bf16[2304,256]{1,0:T(8,128)(2,1)})) %all-reduce.9.cloned.1.call-update) | async-done | bytes 2359312 | tf_op jit(solution)/shard_map/psum | solution.py:9
  77.6 0.0 copy-start.3
  77.7 7.3 %fusion = f32[256,2304]{1,0:T(8,128)S(1)} fusion(bf16[2304,4608]{1,0:T(8,128)(2,1)} %param.4, bf16[2304,256]{1,0:T(8,128)(2,1)} %get-tuple-element.4, f32[2304]{0:T(1024)S(1)} %get-tuple-element.9), kind=kOutput, calls=%fused_computation | convolution fusion | flops 2719678464 | bytes 14164992 | tf_op jit(solution)/shard_map/dot_general | solution.py:32
  85.0 0.0 copy-done.3
  85.0 8.9 %fusion.7 = f32[2304,256]{0,1:T(8,128)} fusion(f32[256,2304]{1,0:T(8,128)S(1)} %fusion, bf16[2304,4608]{1,0:T(8,128)(2,1)} %param.4, bf16[2304,256]{1,0:T(8,128)(2,1)S(1)} %copy-done.3, f32[2304]{0:T(1024)S(1)} %get-tuple-element.8), kind=kOutput, calls=%fused_computation.5 | convolution fusion | flops 2720268288 | bytes 16524288 | tf_op jit(solution)/shard_map/dot_general | solution.py:32
  93.9 0.0 copy-start.1
  93.9 0.0 all-reduce.5.cloned.1.call-update
  93.9 0.0 all-reduce.7.cloned.1.call-start
  94.0 1.2 copy-done.1
  95.2 0.7 copy.6
  95.9 0.1 dynamic-slice_convert_fusion.1
  96.0 92.0 %all-reduce.5.cloned.1.call-done = f32[2304,256]{0,1:T(8,128)} async-done(((f32[2304,256]{0,1:T(8,128)}), f32[2304,256]{0,1:T(8,128)}) %all-reduce.5.cloned.1.call-update) | async-done | bytes 2359312 | tf_op jit(solution)/shard_map/psum | solution.py:37
  188.0 4.7 %fusion.10 = f32[256,256]{1,0:T(8,128)} fusion(bf16[2304,256]{0,1:T(8,128)(2,1)S(1)} %copy.6, f32[2304]{0:T(1024)S(1)} %dynamic-slice_convert_fusion.1, f32[2304,256]{0,1:T(8,128)} %all-reduce.5.cloned.1.call-done), kind=kOutput, calls=%fused_computation.6 | convolution fusion | flops 1814298624 | bytes 3810304 | tf_op jit(solution)/shard_map/dot_general | solution.py:39
  192.7 0.0 all-reduce.7.cloned.1.call-update
  192.7 1.8 negate_multiply_fusion
  194.6 0.0 copy-start.2
  194.6 2.0 copy.7
  196.5 49.3 %all-reduce.7.cloned.1.call-done = f32[256,256]{1,0:T(8,128)} async-done(((f32[256,256]{1,0:T(8,128)}), f32[256,256]{1,0:T(8,128)}) %all-reduce.7.cloned.1.call-update) | async-done | bytes 262160 | tf_op jit(solution)/shard_map/psum | solution.py:42
  245.8 0.0 copy-done.2
  245.8 1.7 sub.3
  (2 shorter events, 0.0 us)
Async XLA Ops:
  7.2 3.0 %copy-start = (s32[72]{0:T(128)S(1)}, s32[72]{0:T(128)}, u32[]{:S(2)}) copy-start(s32[72]{0:T(128)} %param.7) | copy-start | bytes 868
  7.2 70.5 %all-reduce.9.cloned.1.call-start = ((), (), s32[]{:S(2)}) async-start(), calls=%async_computation.2 | async-start | bytes 4718592 | tf_op jit(solution)/shard_map/psum | solution.py:9
  10.1 177.9 %all-reduce.5.cloned.1.call-start = ((), (), s32[]{:S(2)}) async-start(), calls=%async_computation | async-start | bytes 4718592 | tf_op jit(solution)/shard_map/psum | solution.py:37
  77.6 7.3 %copy-start.3 = (bf16[2304,256]{1,0:T(8,128)(2,1)S(1)}, bf16[2304,256]{1,0:T(8,128)(2,1)}, u32[]{:S(2)}) copy-start(bf16[2304,256]{1,0:T(8,128)(2,1)} %get-tuple-element.5) | copy-start | bytes 3538948
  93.9 1.3 copy-start.1
  93.9 151.9 %all-reduce.7.cloned.1.call-start = ((), (), s32[]{:S(2)}) async-start(), calls=%async_computation.1 | async-start | bytes 524288 | tf_op jit(solution)/shard_map/psum | solution.py:42
  194.6 51.2 %copy-start.2 = (f32[256,256]{1,0:T(8,128)S(1)}, f32[256,256]{1,0:T(8,128)}, u32[]{:S(2)}) copy-start(f32[256,256]{1,0:T(8,128)} %param.6) | copy-start | bytes 786436
Sparse Core Ops, SparseCore 0:
  11.9 65.7 all-reduce.8
  94.0 93.9 all-reduce.4
  192.9 52.9 all-reduce.6
where the time goes:
time: 254 us
  waiting for transfers between devices  209 us (82%)
  matrix products  20.9 us (8%)
  between operations  13.8 us (5%)
  other arithmetic  6.55 us (3%)
  local copies, waits for them, and re-layouts  4.01 us (2%)
    psum x1, waiting for transfers between devices, per_device(): total = lax.psum(partial_sum, 'pcol')  92 us
    psum x1, waiting for transfers between devices, from_root(): return lax.psum(block, axis)  67.3 us
    psum x1, waiting for transfers between devices, per_device(): diag_total = lax.psum(term, 'prow')  49.3 us
    dot_general x2, matrix products, per_device(): jnp.dot(tile_cols, masked_half, preferred_element_type=jnp.float32)  16.2 us
  transfers between devices with their start and end apart: 3, of which 3 were waited for; matrix products, arithmetic and copies ran while one was open for 2% of the time, Pallas kernels for 0%

commit v1 on v0

--- a/solution.py
+++ b/solution.py
@@ -34,7 +34,9 @@
         )
     local_panel = panel.astype(jnp.float32) * row_live[:, None]
     contract_rows = (((0,), (0,)), ((), ()))
-    total = lax.psum(partial_sum, "pcol")
+    total = partial_sum
+    for hop in (1, 2):
+        total = total + lax.ppermute(total, "pcol", [(dev, dev ^ hop) for dev in range(4)])
     column_inverse = -total * row_live[:, None]
     term = lax.dot_general(
         local_panel, column_inverse, contract_rows, precision=lax.Precision.HIGHEST

time: 254 us -> 316 us (1.24)
  waiting for transfers between devices: 209 us -> 269 us
  starting transfers between devices: 0.12 us -> 4.1 us
  matrix products: 20.9 us -> 17.2 us
    ppermute x0 -> x2, waiting for transfers between devices: none -> 148 us  [per_device(): lax.ppermute(total, 'pcol', [(dev, dev ^ hop) for dev in range(4)])]
    psum x1 -> x0, waiting for transfers between devices: 92 us -> none  [per_device(): total = lax.psum(partial_sum, 'pcol')]
    ppermute x0 -> x2, starting transfers between devices: none -> 4.02 us  [per_device(): lax.ppermute(total, 'pcol', [(dev, dev ^ hop) for dev in range(4)])]
    psum x1, waiting for transfers between devices: 49.3 us -> 52.9 us  [per_device(): diag_total = lax.psum(term, 'prow')]
  transfers between devices with their start and end apart: 3 -> 4, of which waited for: 3 -> 4; matrix products, arithmetic and copies ran while one was open for 2% -> 1% of each run, Pallas kernels for 0% -> 0%
where the time goes in v1:
time: 316 us
  waiting for transfers between devices  269 us (85%)
  matrix products  17.2 us (5%)
  between operations  14.2 us (4%)
  other arithmetic  8.3 us (3%)
  starting transfers between devices  4.1 us (1%)
  local copies, waits for them, and re-layouts  3.64 us (1%)
    ppermute x2, waiting for transfers between devices, per_device(): lax.ppermute(total, 'pcol', [(dev, dev ^ hop) for dev in range(4)])  148 us
    psum x1, waiting for transfers between devices, from_root(): return lax.psum(block, axis)  67.2 us
    psum x1, waiting for transfers between devices, per_device(): diag_total = lax.psum(term, 'prow')  52.9 us
    dot_general x2, matrix products, per_device(): jnp.dot(tile_cols, masked_half, preferred_element_type=jnp.float32)  14.3 us
  transfers between devices with their start and end apart: 4, of which 4 were waited for; matrix products, arithmetic and copies ran while one was open for 1% of the time, Pallas kernels for 0%

profile of v1, /device:TPU:0, one launch (start us, length us, event | category | flops | bytes accessed | tf_op | source)
XLA Modules:
  0.0 316.1 jit_solution(18272764766984340585)
XLA Ops:
  7.2 0.0 copy-start
  7.2 0.0 all-reduce.6.cloned.1.call-start
  7.2 2.9 broadcast_select_fusion.1
  10.1 0.0 all-reduce.6.cloned.1.call-update
  10.1 0.0 all-reduce.4.cloned.1.call-start
  10.2 0.0 copy-done
  10.2 0.1 broadcast_bitcast_fusion
  10.3 0.0 copy-start.5
  10.3 0.1 dynamic-slice_convert_fusion
  10.4 67.2 %all-reduce.6.cloned.1.call-done = (bf16[2304,256]{1,0:T(8,128)(2,1)}, bf16[2304,256]{1,0:T(8,128)(2,1)}) async-done(((bf16[2304,256]{1,0:T(8,128)(2,1)}, bf16[2304,256]{1,0:T(8,128)(2,1)}), (bf16[2304,256]{1,0:T(8,128)(2,1)}, bf16[2304,256]{1,0:T(8,128)(2,1)})) %all-reduce.6.cloned.1.call-update) | async-done | bytes 2359312 | tf_op jit(solution)/shard_map/psum | solution.py:9
  77.6 0.0 copy-start.6
  77.7 7.3 %fusion = f32[256,2304]{1,0:T(8,128)S(1)} fusion(bf16[2304,4608]{1,0:T(8,128)(2,1)} %param.4, bf16[2304,256]{1,0:T(8,128)(2,1)} %get-tuple-element.4, f32[2304]{0:T(1024)S(1)} %get-tuple-element.9), kind=kOutput, calls=%fused_computation | convolution fusion | flops 2719678464 | bytes 14164992 | tf_op jit(solution)/shard_map/dot_general | solution.py:32
  85.0 0.0 copy-done.5
  85.0 0.0 copy-done.6
  85.0 7.0 %fusion.7 = f32[2304,256]{0,1:T(8,128)S(1)} fusion(f32[256,2304]{1,0:T(8,128)S(1)} %fusion, bf16[2304,4608]{1,0:T(8,128)(2,1)} %param.4, bf16[2304,256]{1,0:T(8,128)(2,1)S(1)} %copy-done.6, f32[2304]{0:T(1024)S(1)} %get-tuple-element.8), kind=kOutput, calls=%fused_computation.5 | convolution fusion | flops 2720268288 | bytes 16524288 | tf_op jit(solution)/shard_map/dot_general | solution.py:32
  92.0 0.0 copy-start.2
  92.0 1.5 collective-permute-start
  93.6 50.5 %collective-permute-done = f32[2304,256]{0,1:T(8,128)S(1)} collective-permute-done((f32[2304,256]{0,1:T(8,128)S(1)}, f32[2304,256]{0,1:T(8,128)S(1)}, u32[]{:S(2)}, u32[]{:S(2)}) %collective-permute-start) | collective-permute-done | bytes 2359328 | tf_op jit(solution)/shard_map/ppermute | solution.py:39
  144.1 0.2 add.31
  144.3 0.0 copy-start.1
  144.3 2.5 collective-permute-start.1
  146.8 0.0 copy-done.2
  146.8 1.5 copy.6
  148.3 0.8 dynamic-slice_convert_fusion.1
  149.1 0.0 copy-done.1
  149.1 0.0 copy-start.3
  149.1 97.9 %collective-permute-done.1 = f32[2304,256]{0,1:T(8,128)} collective-permute-done((f32[2304,256]{0,1:T(8,128)S(1)}, f32[2304,256]{0,1:T(8,128)}, u32[]{:S(2)}, u32[]{:S(2)}) %collective-permute-start.1) | collective-permute-done | bytes 2359328 | tf_op jit(solution)/shard_map/ppermute | solution.py:39
  247.1 2.6 negate_multiply_fusion
  249.7 0.0 copy-done.3
  249.7 2.9 fusion.10
  252.6 0.0 all-reduce.4.cloned.1.call-update
  252.6 0.0 copy-start.4
  252.7 2.0 copy.7
  254.6 52.9 %all-reduce.4.cloned.1.call-done = f32[256,256]{1,0:T(8,128)} async-done(((f32[256,256]{1,0:T(8,128)}), f32[256,256]{1,0:T(8,128)}) %all-reduce.4.cloned.1.call-update) | async-done | bytes 262160 | tf_op jit(solution)/shard_map/psum | solution.py:44
  307.5 0.0 copy-done.4
  307.5 1.7 sub.3
  (2 shorter events, 0.0 us)
Async XLA Ops:
  7.2 3.0 copy-start
  7.2 70.5 %all-reduce.6.cloned.1.call-start = ((), (), s32[]{:S(2)}) async-start(), calls=%async_computation.1 | async-start | bytes 4718592 | tf_op jit(solution)/shard_map/psum | solution.py:9
  10.1 297.4 %all-reduce.4.cloned.1.call-start = ((), (), s32[]{:S(2)}) async-start(), calls=%async_computation | async-start | bytes 524288 | tf_op jit(solution)/shard_map/psum | solution.py:44
  10.3 74.7 %copy-start.5 = (s32[9,2,8,128]{3,1,2,0:T(2,128)}, s32[9,2,8,128]{3,1,2,0:T(2,128)S(1)}, u32[]{:S(2)}) copy-start(s32[9,2,8,128]{3,1,2,0:T(2,128)S(1)} %copy.8) | copy-start | bytes 221188
  77.6 7.3 %copy-start.6 = (bf16[2304,256]{1,0:T(8,128)(2,1)S(1)}, bf16[2304,256]{1,0:T(8,128)(2,1)}, u32[]{:S(2)}) copy-start(bf16[2304,256]{1,0:T(8,128)(2,1)} %get-tuple-element.5) | copy-start | bytes 3538948
  92.0 54.8 %copy-start.2 = (bf16[2304,256]{1,0:T(8,128)(2,1)S(1)}, bf16[2304,256]{1,0:T(8,128)(2,1)}, u32[]{:S(2)}) copy-start(bf16[2304,256]{1,0:T(8,128)(2,1)} %param.5) | copy-start | bytes 3538948
  92.0 52.0 %collective-permute-start = (f32[2304,256]{0,1:T(8,128)S(1)}, f32[2304,256]{0,1:T(8,128)S(1)}, u32[]{:S(2)}, u32[]{:S(2)}) collective-permute-start(f32[2304,256]{0,1:T(8,128)S(1)} %fusion.7), channel_id=1, source_target_pairs={{0,1},{1,0},{2,3},{3,2},{4,5},{5,4},{6,7},{7,6},{8,9},{9,8},{10,11... | collective-permute-start | bytes 7077896 | tf_op jit(solution)/shard_map/ppermute | solution.py:39
  144.3 4.8 %copy-start.1 = (f32[2304,256]{0,1:T(8,128)}, f32[2304,256]{0,1:T(8,128)S(1)}, u32[]{:S(2)}) copy-start(f32[2304,256]{0,1:T(8,128)S(1)} %add.31) | copy-start | bytes 7077892
  144.3 102.8 %collective-permute-start.1 = (f32[2304,256]{0,1:T(8,128)S(1)}, f32[2304,256]{0,1:T(8,128)}, u32[]{:S(2)}, u32[]{:S(2)}) collective-permute-start(f32[2304,256]{0,1:T(8,128)S(1)} %add.31), channel_id=1, source_target_pairs={{0,2},{1,3},{2,0},{3,1},{4,6},{5,7},{6,4},{7,5},{8,10},{9,11},{10,... | collective-permute-start | bytes 7077896 | tf_op jit(solution)/shard_map/ppermute | solution.py:39
  149.1 100.6 %copy-start.3 = (bf16[2304,256]{0,1:T(8,128)(2,1)S(1)}, bf16[2304,256]{0,1:T(8,128)(2,1)}, u32[]{:S(2)}) copy-start(bf16[2304,256]{0,1:T(8,128)(2,1)} %copy.6) | copy-start | bytes 3538948
  252.6 54.9 %copy-start.4 = (f32[256,256]{1,0:T(8,128)S(1)}, f32[256,256]{1,0:T(8,128)}, u32[]{:S(2)}) copy-start(f32[256,256]{1,0:T(8,128)} %param.6) | copy-start | bytes 786436
Sparse Core Ops, SparseCore 0:
  11.9 65.7 all-reduce.5
  252.8 54.7 all-reduce.3
